TPU v7x, 512 devices: a whole 4x4x16 slice. The times are simulated.
512 devices in a mesh: dp: 32 (over z, core), seq: 16 (over y, x).
Axes of the slice: x: 4, y: 4, z: 16, core: 2. Of those that a mesh axis runs over, the one named last changes fastest.
Arguments:
- q_pre: bfloat16 [32, 2048, 16, 128], P('dp', 'seq'), may hold values from -6 to 6
- k_pre: bfloat16 [32, 2048, 8, 128], P('dp', 'seq'), may hold values from -6 to 6
- values: bfloat16 [32, 2048, 8, 128], P('dp', 'seq'), may hold values from -6 to 6
- grad_out: bfloat16 [32, 2048, 16, 128], P('dp', 'seq'), may hold values from -6 to 6
- segment_ids: int32 [32, 2048], P('dp', 'seq'), may hold values from 0 to 7, never falling along the last dimension, each value on 1 to 1024 neighbouring positions
- q_gain: float32 [128], replicated, may hold values from 0.1 to 1.9
- k_gain: float32 [128], replicated, may hold values from 0.1 to 1.9
Outputs:
- grad_q: bfloat16 [32, 2048, 16, 128], P('dp', 'seq')
- grad_k: bfloat16 [32, 2048, 8, 128], P('dp', 'seq')
- grad_v: bfloat16 [32, 2048, 8, 128], P('dp', 'seq')
- grad_q_gain: float32 [128], replicated
- grad_k_gain: float32 [128], replicated
Inputs may be any that keep to these rules, and one draw needn't show every extreme that they name: `segment_ids`: along a span the ids never fall, and each id from 0 to 7 names one run of consecutive tokens.
All inputs are finite; a program needn't handle non-finite values.
Results may differ from a plain program's by a relative error of at most 0.017.
Values may be sent and summed in bfloat16 or wider, within the bound.
A program may use at most 64 MiB of HBM per device.

v0:
```python
import jax
import jax.numpy as jnp
from jax import lax
from jax.sharding import PartitionSpec as P

PRESCALE = 168
DOCS = 8
norm_epsilon = 1e-06
rope_base = 1000000.0
rope_factor = 8.0


def document_positions(segments, docs):
    labels = jnp.arange(docs, dtype=jnp.int32)
    member = (segments[:, None] == labels[None, :]).astype(jnp.int32)
    counts = jnp.sum(member, axis=0)
    starts = jnp.cumsum(counts) - counts
    first = jnp.sum(member * starts[None, :], axis=1)
    return (jnp.arange(segments.shape[0], dtype=jnp.int32) - first, first)


def embed(rows, gain, positions):
    width = rows.shape[-1]
    half = width // 2
    scale = lax.rsqrt(jnp.mean(rows * rows, axis=-1, keepdims=True) + norm_epsilon)
    normed = rows * scale * gain
    freqs = rope_base ** (-(jnp.arange(half, dtype=jnp.float32) * 2.0 / width))
    angles = (positions.astype(jnp.float32) / rope_factor)[:, None] * freqs[None, :]
    cosine = jnp.cos(angles)[:, None, :]
    sine = jnp.sin(angles)[:, None, :]
    first_half = normed[..., :half]
    second_half = normed[..., half:]
    return jnp.concatenate(
        [first_half * cosine - second_half * sine, second_half * cosine + first_half * sine],
        axis=-1,
    )


def attend_blocks(queries, keys, vals, upstream, segments):
    total = queries.shape[0]
    group = queries.shape[1]
    width = queries.shape[2]
    block = min(512, total)
    count = total // block
    rows = block * group
    score_scale = float(PRESCALE) ** (-0.5)
    contract_last = (((1,), (1,)), ((), ()))
    contract_first = (((0,), (0,)), ((), ()))

    def query_block(query_index, carry):
        query_grads, key_grads, value_grads = carry
        start = query_index * block
        query_rows = lax.dynamic_slice_in_dim(queries, start, block, 0).reshape(rows, width)
        upstream_rows = lax.dynamic_slice_in_dim(upstream, start, block, 0).reshape(rows, width)
        query_segs = jnp.repeat(lax.dynamic_slice_in_dim(segments, start, block, 0), group)
        query_places = jnp.repeat(start + jnp.arange(block, dtype=jnp.int32), group)
        lower = 0

        def key_scores(key_index):
            key_start = key_index * block
            key_rows = lax.dynamic_slice_in_dim(keys, key_start, block, 0)
            value_rows = lax.dynamic_slice_in_dim(vals, key_start, block, 0)
            key_segs = lax.dynamic_slice_in_dim(segments, key_start, block, 0)
            key_places = key_start + jnp.arange(block, dtype=jnp.int32)
            scores = score_scale * lax.dot_general(
                query_rows, key_rows, contract_last, preferred_element_type=jnp.float32
            )
            visible = (query_segs[:, None] == key_segs[None, :]) & (
                query_places[:, None] >= key_places[None, :]
            )
            return (scores, visible, key_rows, value_rows, key_start)

        def forward_step(key_index, state):
            totals, numer = state
            scores, visible, key_rows, value_rows, key_start = key_scores(key_index)
            raw = jnp.where(visible, jnp.exp(scores), 0.0)
            numer = numer + jnp.dot(
                raw.astype(jnp.bfloat16), value_rows, preferred_element_type=jnp.float32
            )
            return (totals + jnp.sum(raw, axis=1), numer)

        totals, numer = lax.fori_loop(
            lower,
            query_index + 1,
            forward_step,
            (jnp.zeros((rows,), jnp.float32), jnp.zeros((rows, width), jnp.float32)),
        )
        outputs = numer / totals[:, None]
        delta = jnp.sum(upstream_rows.astype(jnp.float32) * outputs, axis=1)
        logsum = jnp.log(totals)

        def backward_step(key_index, state):
            query_part, key_acc, value_acc = state
            scores, visible, key_rows, value_rows, key_start = key_scores(key_index)
            probs = jnp.where(visible, jnp.exp(scores - logsum[:, None]), 0.0).astype(jnp.bfloat16)
            prob_grads = lax.dot_general(
                upstream_rows, value_rows, contract_last, preferred_element_type=jnp.float32
            )
            score_grads = (
                probs.astype(jnp.float32) * (prob_grads - delta[:, None]) * score_scale
            ).astype(jnp.bfloat16)
            query_part = query_part + jnp.dot(
                score_grads, key_rows, preferred_element_type=jnp.float32
            )
            key_part = lax.dot_general(
                score_grads, query_rows, contract_first, preferred_element_type=jnp.float32
            )
            value_part = lax.dot_general(
                probs, upstream_rows, contract_first, preferred_element_type=jnp.float32
            )
            key_acc = lax.dynamic_update_slice_in_dim(
                key_acc,
                lax.dynamic_slice_in_dim(key_acc, key_start, block, 0) + key_part,
                key_start,
                0,
            )
            value_acc = lax.dynamic_update_slice_in_dim(
                value_acc,
                lax.dynamic_slice_in_dim(value_acc, key_start, block, 0) + value_part,
                key_start,
                0,
            )
            return (query_part, key_acc, value_acc)

        query_part, key_grads, value_grads = lax.fori_loop(
            lower,
            query_index + 1,
            backward_step,
            (jnp.zeros((rows, width), jnp.float32), key_grads, value_grads),
        )
        query_grads = lax.dynamic_update_slice_in_dim(query_grads, query_part, start * group, 0)
        return (query_grads, key_grads, value_grads)

    initial = (
        jnp.zeros((total * group, width), jnp.float32),
        jnp.zeros((total, width), jnp.float32),
        jnp.zeros((total, width), jnp.float32),
    )
    query_grads, key_grads, value_grads = lax.fori_loop(0, count, query_block, initial)
    return (query_grads.reshape(total, group, width), key_grads, value_grads)


def body(q_pre, k_pre, values, grad_out, segment_ids, q_gain, k_gain):
    segments = lax.all_gather(segment_ids, "seq", axis=1, tiled=True)[0]
    positions, first = document_positions(segments, DOCS)
    local = q_pre.shape[1]
    heads = q_pre.shape[2]
    kv_heads = k_pre.shape[2]
    width = q_pre.shape[3]
    group = heads // kv_heads

    def embed_rows(rows, gain):
        return embed(rows, gain, positions)

    key_copies = jnp.repeat(k_pre[0], group, axis=1)
    value_copies = jnp.repeat(values[0], group, axis=1)
    query_here, upstream_here, key_here, value_here = (
        lax.all_to_all(q_pre[0], "seq", split_axis=1, concat_axis=0, tiled=True),
        lax.all_to_all(grad_out[0], "seq", split_axis=1, concat_axis=0, tiled=True),
        lax.all_to_all(key_copies, "seq", split_axis=1, concat_axis=0, tiled=True),
        lax.all_to_all(value_copies, "seq", split_axis=1, concat_axis=0, tiled=True),
    )
    query_rot, query_back = jax.vjp(embed_rows, query_here.astype(jnp.float32), q_gain)
    key_rot, key_back = jax.vjp(embed_rows, key_here.astype(jnp.float32), k_gain)
    query_hat = query_rot.astype(jnp.bfloat16)
    key_hat = key_rot.astype(jnp.bfloat16)
    query_list, key_list, value_list = ([], [], [])
    query_part, key_part, value_part = attend_blocks(
        query_hat, key_hat[:, 0], value_here[:, 0], upstream_here, segments
    )
    query_list.append(query_part)
    key_list.append(key_part)
    value_list.append(value_part)
    query_input, query_gain_part = query_back(query_list[0])
    key_input, key_gain_part = key_back(jnp.stack(key_list, axis=1))
    value_input = jnp.stack(value_list, axis=1)
    query_return, key_return, value_return = (
        lax.all_to_all(
            query_input.astype(jnp.bfloat16), "seq", split_axis=0, concat_axis=1, tiled=True
        ).astype(query_input.dtype),
        lax.all_to_all(
            key_input.astype(jnp.bfloat16), "seq", split_axis=0, concat_axis=1, tiled=True
        ).astype(key_input.dtype),
        lax.all_to_all(
            value_input.astype(jnp.bfloat16), "seq", split_axis=0, concat_axis=1, tiled=True
        ).astype(value_input.dtype),
    )
    grad_q = query_return.astype(jnp.bfloat16)
    grad_k = jnp.sum(key_return.reshape(local, kv_heads, group, width), axis=2).astype(jnp.bfloat16)
    grad_v = jnp.sum(value_return.reshape(local, kv_heads, group, width), axis=2).astype(
        jnp.bfloat16
    )
    gain_totals = lax.psum((query_gain_part, key_gain_part), ("dp", "seq"))
    return (grad_q[None], grad_k[None], grad_v[None], gain_totals[0], gain_totals[1])


def solution(mesh):
    return jax.shard_map(
        body,
        mesh=mesh,
        in_specs=(
            P("dp", "seq", None, None),
            P("dp", "seq", None, None),
            P("dp", "seq", None, None),
            P("dp", "seq", None, None),
            P("dp", "seq"),
            P(),
            P(),
        ),
        out_specs=(
            P("dp", "seq", None, None),
            P("dp", "seq", None, None),
            P("dp", "seq", None, None),
            P(),
            P(),
        ),
        check_vma=False,
    )
```

profile of v0, /device:TPU:1, one launch (start us, length us, event | category | flops | bytes accessed | tf_op | source)
XLA Modules:
  0.0 308.5 jit_solution(509402824562934716)
XLA Ops:
  0.6 2.0 copy.172
  2.6 7.7 %all-to-all-start = ((bf16[128,16,128]{2,0,1:T(8,128)(2,1)}), bf16[128,16,128]{2,0,1:T(8,128)(2,1)S(1)}, u32[]{:S(2)}, u32[]{:S(2)}) async-start(bf16[128,16,128]{2,0,1:T(8,128)(2,1)} %bitcast.130), calls=%async_computation | async-start | bytes 1048576 | tf_op jit(solution)/shard_map/all_to_all | solution.py:158
  10.4 17.6 %all_gather.3 = s32[1,2048]{1,0:T(1,128)S(1)} all-gather(s32[1,128]{1,0:T(1,128)S(1)} %copy-done.13), channel_id=1, replica_groups=mesh['dp'=32,'seq'=16] {'seq'}, dimensions={1}, use_global_device_ids=true | all-gather | bytes 8704 | tf_op jit(solution)/shard_map/all_gather | solution.py:144
  31.3 4.0 %all-to-all-start.1 = ((bf16[128,16,128]{0,2,1:T(8,128)(2,1)}), bf16[128,16,128]{0,2,1:T(8,128)(2,1)S(1)}, u32[]{:S(2)}, u32[]{:S(2)}) async-start(bf16[128,16,128]{0,2,1:T(8,128)(2,1)} %bitcast.12), calls=%async_computation.1 | async-start | bytes 1048576 | tf_op jit(solution)/shard_map/all_to_all | solution.py:160
  37.4 6.9 %all-to-all-done.1 = bf16[128,16,128]{0,2,1:T(8,128)(2,1)S(1)} async-done(((bf16[128,16,128]{0,2,1:T(8,128)(2,1)}), bf16[128,16,128]{0,2,1:T(8,128)(2,1)S(1)}, u32[]{:S(2)}, u32[]{:S(2)}) %all-to-all-start.1) | async-done | bytes 524320 | tf_op jit(solution)/shard_map/all_to_all | solution.py:160
  45.3 3.6 %all-to-all-start.2 = ((bf16[128,16,128]{2,0,1:T(8,128)(2,1)}), bf16[128,16,128]{2,0,1:T(8,128)(2,1)S(1)}, u32[]{:S(2)}, u32[]{:S(2)}) async-start(bf16[128,16,128]{2,0,1:T(8,128)(2,1)} %bitcast.20), calls=%async_computation.2 | async-start | bytes 1048576 | tf_op jit(solution)/shard_map/all_to_all | solution.py:161
  49.6 1.2 fusion.33
  50.8 7.0 %all-to-all-done.2 = bf16[128,16,128]{2,0,1:T(8,128)(2,1)S(1)} async-done(((bf16[128,16,128]{2,0,1:T(8,128)(2,1)}), bf16[128,16,128]{2,0,1:T(8,128)(2,1)S(1)}, u32[]{:S(2)}, u32[]{:S(2)}) %all-to-all-start.2) | async-done | bytes 524320 | tf_op jit(solution)/shard_map/all_to_all | solution.py:161
  57.8 4.2 %all-to-all-start.3 = ((bf16[128,16,128]{2,0,1:T(8,128)(2,1)}), bf16[128,16,128]{2,0,1:T(8,128)(2,1)}, u32[]{:S(2)}, u32[]{:S(2)}) async-start(bf16[128,16,128]{2,0,1:T(8,128)(2,1)} %bitcast.129), calls=%async_computation.3 | async-start | bytes 1048576 | tf_op jit(solution)/shard_map/all_to_all | solution.py:159
  62.1 3.1 fusion.63
  66.2 4.8 %all-to-all-done.3 = bf16[128,16,128]{2,0,1:T(8,128)(2,1)} async-done(((bf16[128,16,128]{2,0,1:T(8,128)(2,1)}), bf16[128,16,128]{2,0,1:T(8,128)(2,1)}, u32[]{:S(2)}, u32[]{:S(2)}) %all-to-all-start.3) | async-done | bytes 524320 | tf_op jit(solution)/shard_map/all_to_all | solution.py:159
  71.1 1.1 broadcast.338.clone
  72.3 69.1 %while.79 = (s32[]{:T(128)}, f32[2048,128]{0,1:T(8,128)}, f32[2048,128]{1,0:T(8,128)S(1)}, f32[2048,128]{1,0:T(8,128)S(1)}, bf16[2048,1,128]{0,2,1:T(8,128)(2,1)...) while((s32[]{:T(128)}, f32[2048,128]{0,1:T(8,128)}, ...), condition=%wide.region_12.13_spmd, body=%wide.region_5.12_spmd.sunk | while | flops 475268608 | bytes 14478353 | solution.py:139
  73.2 1.9 while.80
  73.3 1.4 fusion.101
  75.1 1.1 multiply_reduce_fusion.6
  76.3 3.7 %while.81 = (s32[]{:T(128)}, f32[512,128]{1,0:T(8,128)S(1)}, f32[2048,128]{1,0:T(8,128)S(1)}, f32[2048,128]{1,0:T(8,128)S(1)}, s32[]{:T(128)}, /*index=5*/s32[51...) while((s32[]{:T(128)}, f32[512,128]{1,0:T(8,128)S(1)}, ...), condition=%wide.region_11.11_spmd.clone, body=%wide.region_10.10_spmd.clone.sunk | while | flops 338887680 | bytes 5656819 | solution.py:125
  76.4 1.4 fusion.112
  78.7 1.3 convolution_add_fusion.7
  82.1 3.7 %while.80 = (s32[]{:T(128)}, f32[512]{0:T(512)S(1)}, f32[512,128]{1,0:T(8,128)S(1)}, s32[]{:T(128)}, s32[512]{0:T(512)S(1)}, /*index=5*/s32[2048]{0:T(1024)S(1)}...) while((s32[]{:T(128)}, f32[512]{0:T(512)S(1)}, ...), condition=%wide.region_8.8_spmd.clone, body=%wide.region_6.7_spmd.clone.sunk | while | flops 136119296 | bytes 1990855 | solution.py:82
  82.2 1.4 fusion.101
  84.1 1.4 fusion.101
  85.9 1.1 multiply_reduce_fusion.6
  87.0 7.4 %while.81 = (s32[]{:T(128)}, f32[512,128]{1,0:T(8,128)S(1)}, f32[2048,128]{1,0:T(8,128)S(1)}, f32[2048,128]{1,0:T(8,128)S(1)}, s32[]{:T(128)}, /*index=5*/s32[51...) while((s32[]{:T(128)}, f32[512,128]{1,0:T(8,128)S(1)}, ...), condition=%wide.region_11.11_spmd.clone, body=%wide.region_10.10_spmd.clone.sunk | while | flops 338887680 | bytes 5656819 | solution.py:125
  87.1 1.4 fusion.112
  89.5 1.3 convolution_add_fusion.7
  90.9 1.4 fusion.112
  93.2 1.3 convolution_add_fusion.7
  96.6 5.6 %while.80 = (s32[]{:T(128)}, f32[512]{0:T(512)S(1)}, f32[512,128]{1,0:T(8,128)S(1)}, s32[]{:T(128)}, s32[512]{0:T(512)S(1)}, /*index=5*/s32[2048]{0:T(1024)S(1)}...) while((s32[]{:T(128)}, f32[512]{0:T(512)S(1)}, ...), condition=%wide.region_8.8_spmd.clone, body=%wide.region_6.7_spmd.clone.sunk | while | flops 136119296 | bytes 1990855 | solution.py:82
  96.7 1.4 fusion.101
  98.6 1.4 fusion.101
  100.4 1.4 fusion.101
  102.2 1.1 multiply_reduce_fusion.6
  103.4 11.1 %while.81 = (s32[]{:T(128)}, f32[512,128]{1,0:T(8,128)S(1)}, f32[2048,128]{1,0:T(8,128)S(1)}, f32[2048,128]{1,0:T(8,128)S(1)}, s32[]{:T(128)}, /*index=5*/s32[51...) while((s32[]{:T(128)}, f32[512,128]{1,0:T(8,128)S(1)}, ...), condition=%wide.region_11.11_spmd.clone, body=%wide.region_10.10_spmd.clone.sunk | while | flops 338887680 | bytes 5656819 | solution.py:125
  103.5 1.4 fusion.112
  105.8 1.3 convolution_add_fusion.7
  107.2 1.4 fusion.112
  109.5 1.3 convolution_add_fusion.7
  110.9 1.4 fusion.112
  113.2 1.3 convolution_add_fusion.7
  116.6 7.5 %while.80 = (s32[]{:T(128)}, f32[512]{0:T(512)S(1)}, f32[512,128]{1,0:T(8,128)S(1)}, s32[]{:T(128)}, s32[512]{0:T(512)S(1)}, /*index=5*/s32[2048]{0:T(1024)S(1)}...) while((s32[]{:T(128)}, f32[512]{0:T(512)S(1)}, ...), condition=%wide.region_8.8_spmd.clone, body=%wide.region_6.7_spmd.clone.sunk | while | flops 136119296 | bytes 1990855 | solution.py:82
  116.7 1.4 fusion.101
  118.6 1.4 fusion.101
  120.5 1.4 fusion.101
  122.3 1.4 fusion.101
  124.1 1.1 multiply_reduce_fusion.6
  125.3 14.8 %while.81 = (s32[]{:T(128)}, f32[512,128]{1,0:T(8,128)S(1)}, f32[2048,128]{1,0:T(8,128)S(1)}, f32[2048,128]{1,0:T(8,128)S(1)}, s32[]{:T(128)}, /*index=5*/s32[51...) while((s32[]{:T(128)}, f32[512,128]{1,0:T(8,128)S(1)}, ...), condition=%wide.region_11.11_spmd.clone, body=%wide.region_10.10_spmd.clone.sunk | while | flops 338887680 | bytes 5656819 | solution.py:125
  125.4 1.4 fusion.112
  127.7 1.3 convolution_add_fusion.7
  129.1 1.4 fusion.112
  131.4 1.3 convolution_add_fusion.7
  132.8 1.4 fusion.112
  135.1 1.3 convolution_add_fusion.7
  136.5 1.4 fusion.112
  138.8 1.3 convolution_add_fusion.7
  141.4 1.3 copy.139
  142.7 4.1 %fusion.60 = (f32[2048,1,64]{0,2,1:T(8,128)S(1)}, f32[2048,1,64]{0,2,1:T(8,128)S(1)}, f32[2048,1,64]{0,2,1:T(8,128)S(1)}, f32[2048,1,64]{0,2,1:T(8,128)S(1)}) fusion(f32[2048,1,128]{0,2,1:T(8,128)} %bitcast.158, f32[64]{0:T(128)S(1)} %negate_power_fusion, f32[2048]{0:T(1024)S(1)} %convert_multiply_fusion.1, f32[2048,1,128]{0,2,1:T(8,128)} %bitcast.157), kind=kLoop, calls=%fused_computation.89 | loop fusion | flops 1966080 | bytes 4202752 | tf_op jit(solution)/shard_map/transpose(jvp())/add_any | solution.py:34
  151.6 3.6 %all-to-all-start.4 = ((bf16[16,2,8192]{2,1,0:T(2,128)(2,1)}), bf16[16,2,8192]{2,1,0:T(2,128)(2,1)S(1)}, u32[]{:S(2)}, u32[]{:S(2)}) async-start(bf16[16,2,8192]{2,1,0:T(2,128)(2,1)} %reshape.576), calls=%async_computation.4 | async-start | bytes 1048576 | tf_op jit(solution)/shard_map/all_to_all | solution.py:178
  157.4 6.8 %all-to-all-done.4 = bf16[16,2,8192]{2,1,0:T(2,128)(2,1)S(1)} async-done(((bf16[16,2,8192]{2,1,0:T(2,128)(2,1)}), bf16[16,2,8192]{2,1,0:T(2,128)(2,1)S(1)}, u32[]{:S(2)}, u32[]{:S(2)}) %all-to-all-start.4) | async-done | bytes 524320 | tf_op jit(solution)/shard_map/all_to_all | solution.py:178
  164.1 3.6 %all-to-all-start.5 = ((bf16[16,2,8192]{2,1,0:T(2,128)(2,1)}), bf16[16,2,8192]{2,1,0:T(2,128)(2,1)S(1)}, u32[]{:S(2)}, u32[]{:S(2)}) async-start(bf16[16,2,8192]{2,1,0:T(2,128)(2,1)} %reshape.578), calls=%async_computation.5 | async-start | bytes 1048576 | tf_op jit(solution)/shard_map/all_to_all | solution.py:181
  169.7 9.0 %all-to-all-done.5 = bf16[16,2,8192]{2,1,0:T(2,128)(2,1)S(1)} async-done(((bf16[16,2,8192]{2,1,0:T(2,128)(2,1)}), bf16[16,2,8192]{2,1,0:T(2,128)(2,1)S(1)}, u32[]{:S(2)}, u32[]{:S(2)}) %all-to-all-start.5) | async-done | bytes 524320 | tf_op jit(solution)/shard_map/all_to_all | solution.py:181
  178.7 3.6 %all-to-all-start.6 = ((bf16[16,2,8192]{2,1,0:T(2,128)(2,1)}), bf16[16,2,8192]{2,1,0:T(2,128)(2,1)S(1)}, u32[]{:S(2)}, u32[]{:S(2)}) async-start(bf16[16,2,8192]{2,1,0:T(2,128)(2,1)} %reshape.580), calls=%async_computation.6 | async-start | bytes 1048576 | tf_op jit(solution)/shard_map/all_to_all | solution.py:184
  182.3 121.2 %all-reduce.4 = (f32[128]{0:T(128)}, f32[128]{0:T(128)}) all-reduce(f32[128]{0:T(128)S(1)} %get-tuple-element.430, f32[128]{0:T(128)S(1)} %get-tuple-element.428), channel_id=1, replica_groups=mesh['dp'=32,'seq'=16] {'dp','seq'}, use_global_device_ids=true, to_apply=%region_18.19 | all-reduce | flops 256 | bytes 2048 | tf_op jit(solution)/shard_map/psum | solution.py:193
  304.1 1.1 copy.142
  (216 shorter events, 44.1 us)
Async XLA Ops:
  2.6 7.7 %copy-start.13 = (s32[1,128]{1,0:T(1,128)S(1)}, s32[1,128]{1,0:T(1,128)}, u32[]{:S(2)}) copy-start(s32[1,128]{1,0:T(1,128)} %param.17) | copy-start | bytes 1540
  2.6 25.7 %copy-start.9 = (bf16[1,128,8,128]{3,2,1,0:T(8,128)(2,1)S(1)}, bf16[1,128,8,128]{3,2,1,0:T(8,128)(2,1)}, u32[]{:S(2)}) copy-start(bf16[1,128,8,128]{3,2,1,0:T(8,128)(2,1)} %param.14) | copy-start | bytes 786436
  2.6 27.8 %all-to-all-start = ((bf16[128,16,128]{2,0,1:T(8,128)(2,1)}), bf16[128,16,128]{2,0,1:T(8,128)(2,1)S(1)}, u32[]{:S(2)}, u32[]{:S(2)}) async-start(bf16[128,16,128]{2,0,1:T(8,128)(2,1)} %bitcast.130), calls=%async_computation | async-start | bytes 1048576 | tf_op jit(solution)/shard_map/all_to_all | solution.py:158
  10.3 18.2 %copy-start.10 = (bf16[1,128,8,128]{3,2,1,0:T(8,128)(2,1)S(1)}, bf16[1,128,8,128]{3,2,1,0:T(8,128)(2,1)}, u32[]{:S(2)}) copy-start(bf16[1,128,8,128]{3,2,1,0:T(8,128)(2,1)} %param.15) | copy-start | bytes 786436
  28.3 1.0 copy-start.8
  31.3 13.0 %all-to-all-start.1 = ((bf16[128,16,128]{0,2,1:T(8,128)(2,1)}), bf16[128,16,128]{0,2,1:T(8,128)(2,1)S(1)}, u32[]{:S(2)}, u32[]{:S(2)}) async-start(bf16[128,16,128]{0,2,1:T(8,128)(2,1)} %bitcast.12), calls=%async_computation.1 | async-start | bytes 1048576 | tf_op jit(solution)/shard_map/all_to_all | solution.py:160
  35.8 0.7 copy-start.12
  36.5 1.0 copy-start
  44.3 4.7 %copy-start.2 = (bf16[128,16,128]{0,2,1:T(8,128)(2,1)}, bf16[128,16,128]{0,2,1:T(8,128)(2,1)S(1)}, u32[]{:S(2)}) copy-start(bf16[128,16,128]{0,2,1:T(8,128)(2,1)S(1)} %all-to-all-done.1) | copy-start | bytes 1572868
  45.3 12.5 %all-to-all-start.2 = ((bf16[128,16,128]{2,0,1:T(8,128)(2,1)}), bf16[128,16,128]{2,0,1:T(8,128)(2,1)S(1)}, u32[]{:S(2)}, u32[]{:S(2)}) async-start(bf16[128,16,128]{2,0,1:T(8,128)(2,1)} %bitcast.20), calls=%async_computation.2 | async-start | bytes 1048576 | tf_op jit(solution)/shard_map/all_to_all | solution.py:161
  49.0 0.7 copy-start.11
  50.8 11.2 %copy-start.4 = (f32[2048,1,128]{0,2,1:T(8,128)S(1)}, f32[2048,1,128]{0,2,1:T(8,128)}, u32[]{:S(2)}) copy-start(f32[2048,1,128]{0,2,1:T(8,128)} %fusion.33) | copy-start | bytes 3145732
  57.8 13.2 %all-to-all-start.3 = ((bf16[128,16,128]{2,0,1:T(8,128)(2,1)}), bf16[128,16,128]{2,0,1:T(8,128)(2,1)}, u32[]{:S(2)}, u32[]{:S(2)}) async-start(bf16[128,16,128]{2,0,1:T(8,128)(2,1)} %bitcast.129), calls=%async_computation.3 | async-start | bytes 1048576 | tf_op jit(solution)/shard_map/all_to_all | solution.py:159
  65.2 1.0 copy-start.7
  72.4 0.8 copy-start.5
  80.1 1.1 copy-start.6
  81.3 0.8 copy-start.5
  94.6 1.1 copy-start.6
  95.7 0.8 copy-start.5
  114.6 1.1 copy-start.6
  115.8 0.8 copy-start.5
  140.3 1.1 copy-start.6
  142.7 4.1 %copy-start.3 = (bf16[128,16,128]{0,2,1:T(8,128)(2,1)S(1)}, bf16[128,16,128]{0,2,1:T(8,128)(2,1)}, u32[]{:S(2)}) copy-start(bf16[128,16,128]{0,2,1:T(8,128)(2,1)} %copy-done.2) | copy-start | bytes 1572868
  146.8 1.2 copy-start.1
  151.6 12.5 %all-to-all-start.4 = ((bf16[16,2,8192]{2,1,0:T(2,128)(2,1)}), bf16[16,2,8192]{2,1,0:T(2,128)(2,1)S(1)}, u32[]{:S(2)}, u32[]{:S(2)}) async-start(bf16[16,2,8192]{2,1,0:T(2,128)(2,1)} %reshape.576), calls=%async_computation.4 | async-start | bytes 1048576 | tf_op jit(solution)/shard_map/all_to_all | solution.py:178
  164.1 14.6 %all-to-all-start.5 = ((bf16[16,2,8192]{2,1,0:T(2,128)(2,1)}), bf16[16,2,8192]{2,1,0:T(2,128)(2,1)S(1)}, u32[]{:S(2)}, u32[]{:S(2)}) async-start(bf16[16,2,8192]{2,1,0:T(2,128)(2,1)} %reshape.578), calls=%async_computation.5 | async-start | bytes 1048576 | tf_op jit(solution)/shard_map/all_to_all | solution.py:181
  178.7 128.1 %all-to-all-start.6 = ((bf16[16,2,8192]{2,1,0:T(2,128)(2,1)}), bf16[16,2,8192]{2,1,0:T(2,128)(2,1)S(1)}, u32[]{:S(2)}, u32[]{:S(2)}) async-start(bf16[16,2,8192]{2,1,0:T(2,128)(2,1)} %reshape.580), calls=%async_computation.6 | async-start | bytes 1048576 | tf_op jit(solution)/shard_map/all_to_all | solution.py:184
where the time goes:
time: 310 us; the launch traced here: 308 us
  blocking collectives  139 us (45%)
  matrix products  53.1 us (17%)
  waiting for transfers between devices  34.4 us (11%)
  local copies, waits for them, and re-layouts  30.6 us (10%)
  starting transfers between devices  30.2 us (10%)
  other arithmetic  19 us (6%)
    psum x1, blocking collectives, body(): gain_totals = lax.psum((query_gain_part, key_gain_part), ('dp', 'seq'))  121 us
    dot_general x20, matrix products, key_scores(): lax.dot_general(query_rows, key_rows, contract_last, preferred_element_ty...  27.3 us
    all_gather x1, blocking collectives, body(): segments = lax.all_gather(segment_ids, 'seq', axis=1, tiled=True)[0]  17.6 us
    unnamed x40, local copies, waits for them, and re-layouts  14.1 us
    dot_general x10, matrix products, backward_step(): jnp.dot(score_grads, key_rows, preferred_element_type=jnp.float32)  12.8 us
    all_to_all x1, waiting for transfers between devices, body(): lax.all_to_all(key_input.astype(jnp.bfloat16), 'seq', split_axis=0, conca...  8.96 us
    all_to_all x1, starting transfers between devices, body(): lax.all_to_all(q_pre[0], 'seq', split_axis=1, concat_axis=0, tiled=True)  7.72 us
    all_to_all x1, waiting for transfers between devices, body(): lax.all_to_all(value_copies, 'seq', split_axis=1, concat_axis=0, tiled=True)  6.98 us
  transfers between devices with their start and end apart: 7, of which 5 were waited for; matrix products, arithmetic and copies ran while one was open for 5% of the time, Pallas kernels for 0%

commit v1 on v0

--- a/solution.py
+++ b/solution.py
@@ -8,6 +8,19 @@
 norm_epsilon = 1e-06
 rope_base = 1000000.0
 rope_factor = 8.0
+
+
+def gather_around(shard, axis, dim):
+    ways = lax.axis_size(axis)
+    up = [(d, (d + 1) % ways) for d in range(ways)]
+    down = [(d, (d - 1) % ways) for d in range(ways)]
+    earlier, later = ([shard], [shard])
+    for _ in range(ways // 2):
+        earlier.append(lax.ppermute(earlier[-1], axis, up))
+    for _ in range((ways - 1) // 2):
+        later.append(lax.ppermute(later[-1], axis, down))
+    line = jnp.concatenate([*earlier[::-1], *later[1:]], axis=dim)
+    return jnp.roll(line, (lax.axis_index(axis) - ways // 2) * shard.shape[dim], axis=dim)
 
 
 def document_positions(segments, docs):
@@ -141,7 +154,7 @@
 
 
 def body(q_pre, k_pre, values, grad_out, segment_ids, q_gain, k_gain):
-    segments = lax.all_gather(segment_ids, "seq", axis=1, tiled=True)[0]
+    segments = gather_around(segment_ids, "seq", 1)[0]
     positions, first = document_positions(segments, DOCS)
     local = q_pre.shape[1]
     heads = q_pre.shape[2]

time: 310 us -> 366 us (1.18)
  starting transfers between devices: 30.2 us -> 95.4 us
  blocking collectives: 139 us -> 121 us
  waiting for transfers between devices: 34.4 us -> 42.2 us
    ppermute x0 -> x15, starting transfers between devices: none -> 64.2 us  [the longest x7 46.8 us: gather_around(): later.append(lax.ppermute(later[-1], axis, down))]
    all_gather x1 -> x0, blocking collectives: 17.6 us -> none  [body(): segments = lax.all_gather(segment_ids, 'seq', axis=1, tiled=True)[0]]
    ppermute x0 -> x15, waiting for transfers between devices: none -> 4.8 us  [the longest x8 4.79 us: gather_around(): earlier.append(lax.ppermute(earlier[-1], axis, up))]
    unnamed x40 -> x71, local copies, waits for them, and re-layouts: 14.1 us -> 14.2 us
  transfers between devices with their start and end apart: 7 -> 22, of which waited for: 5 -> 6; matrix products, arithmetic and copies ran while one was open for 5% -> 5% of each run, Pallas kernels for 0% -> 0%
where the time goes in v1:
time: 366 us; the launch traced here: 364 us
  blocking collectives  121 us (33%)
  starting transfers between devices  95.4 us (26%)
  matrix products  53.1 us (15%)
  waiting for transfers between devices  42.2 us (12%)
  local copies, waits for them, and re-layouts  30.7 us (8%)
  other arithmetic  19 us (5%)
    psum x1, blocking collectives, body(): gain_totals = lax.psum((query_gain_part, key_gain_part), ('dp', 'seq'))  121 us
    ppermute x7, starting transfers between devices, gather_around(): later.append(lax.ppermute(later[-1], axis, down))  46.8 us
    dot_general x20, matrix products, key_scores(): lax.dot_general(query_rows, key_rows, contract_last, preferred_element_ty...  27.3 us
    ppermute x8, starting transfers between devices, gather_around(): earlier.append(lax.ppermute(earlier[-1], axis, up))  17.4 us
    unnamed x71, local copies, waits for them, and re-layouts  14.2 us
    dot_general x10, matrix products, backward_step(): jnp.dot(score_grads, key_rows, preferred_element_type=jnp.float32)  12.8 us
    all_to_all x1, waiting for transfers between devices, body(): lax.all_to_all(value_copies, 'seq', split_axis=1, concat_axis=0, tiled=True)  10.4 us
  transfers between devices with their start and end apart: 22, of which 6 were waited for; matrix products, arithmetic and copies ran while one was open for 5% of the time, Pallas kernels for 0%

profile of v1, /device:TPU:1, one launch (start us, length us, event | category | flops | bytes accessed | tf_op | source)
XLA Modules:
  0.0 363.6 jit_solution(11804515122698345449)
XLA Ops:
  0.6 4.0 %collective-permute-start = (s32[1,128]{1,0:T(1,128)}, s32[1,128]{1,0:T(1,128)S(1)}, u32[]{:S(2)}, u32[]{:S(2)}) collective-permute-start(s32[1,128]{1,0:T(1,128)} %param.17), channel_id=1, source_target_pairs={{0,1},{1,2},{2,3},{3,4},{4,5},{5,6},{6,7},{7,8},{8,9},{9,10},{10,1... | collective-permute-start | bytes 1544 | tf_op jit(solution)/shard_map/ppermute | solution.py:19
  4.6 4.8 %collective-permute-done = s32[1,128]{1,0:T(1,128)S(1)} collective-permute-done((s32[1,128]{1,0:T(1,128)}, s32[1,128]{1,0:T(1,128)S(1)}, u32[]{:S(2)}, u32[]{:S(2)}) %collective-permute-start) | collective-permute-done | bytes 544 | tf_op jit(solution)/shard_map/ppermute | solution.py:19
  9.4 1.9 collective-permute-start.1
  11.3 6.7 %collective-permute-start.8 = (s32[1,128]{1,0:T(1,128)}, s32[1,128]{1,0:T(1,128)S(1)}, u32[]{:S(2)}, u32[]{:S(2)}) collective-permute-start(s32[1,128]{1,0:T(1,128)} %param.17), channel_id=1, source_target_pairs={{0,15},{1,0},{2,1},{3,2},{4,3},{5,4},{6,5},{7,6},{8,7},{9,8},{10,9... | collective-permute-start | bytes 1544 | tf_op jit(solution)/shard_map/ppermute | solution.py:21
  18.0 1.9 collective-permute-start.2
  19.9 2.0 copy.172
  21.9 6.3 %all-to-all-start = ((bf16[128,16,128]{2,0,1:T(8,128)(2,1)}), bf16[128,16,128]{2,0,1:T(8,128)(2,1)S(1)}, u32[]{:S(2)}, u32[]{:S(2)}) async-start(bf16[128,16,128]{2,0,1:T(8,128)(2,1)} %bitcast.130), calls=%async_computation | async-start | bytes 1048576 | tf_op jit(solution)/shard_map/all_to_all | solution.py:171
  28.2 6.6 %collective-permute-start.9 = (s32[1,128]{1,0:T(1,128)S(1)}, s32[1,128]{1,0:T(1,128)S(1)}, u32[]{:S(2)}, u32[]{:S(2)}) collective-permute-start(s32[1,128]{1,0:T(1,128)S(1)} %collective-permute-done.8), channel_id=1, source_target_pairs={{0,15},{1,0},{2,1},{3,2},{4,3},{5,4},{6,5},{7,6},{8,7},{9,8},{10,9... | collective-permute-start | bytes 1544 | tf_op jit(solution)/shard_map/ppermute | solution.py:21
  34.8 1.9 collective-permute-start.3
  36.8 6.7 %collective-permute-start.10 = (s32[1,128]{1,0:T(1,128)S(1)}, s32[1,128]{1,0:T(1,128)S(1)}, u32[]{:S(2)}, u32[]{:S(2)}) collective-permute-start(s32[1,128]{1,0:T(1,128)S(1)} %collective-permute-done.9), channel_id=1, source_target_pairs={{0,15},{1,0},{2,1},{3,2},{4,3},{5,4},{6,5},{7,6},{8,7},{9,8},{10,9... | collective-permute-start | bytes 1544 | tf_op jit(solution)/shard_map/ppermute | solution.py:21
  43.5 1.9 collective-permute-start.4
  45.4 6.8 %collective-permute-start.11 = (s32[1,128]{1,0:T(1,128)S(1)}, s32[1,128]{1,0:T(1,128)S(1)}, u32[]{:S(2)}, u32[]{:S(2)}) collective-permute-start(s32[1,128]{1,0:T(1,128)S(1)} %collective-permute-done.10), channel_id=1, source_target_pairs={{0,15},{1,0},{2,1},{3,2},{4,3},{5,4},{6,5},{7,6},{8,7},{9,8},{10,9... | collective-permute-start | bytes 1544 | tf_op jit(solution)/shard_map/ppermute | solution.py:21
  52.2 1.9 collective-permute-start.5
  54.2 6.7 %collective-permute-start.12 = (s32[1,128]{1,0:T(1,128)S(1)}, s32[1,128]{1,0:T(1,128)S(1)}, u32[]{:S(2)}, u32[]{:S(2)}) collective-permute-start(s32[1,128]{1,0:T(1,128)S(1)} %collective-permute-done.11), channel_id=1, source_target_pairs={{0,15},{1,0},{2,1},{3,2},{4,3},{5,4},{6,5},{7,6},{8,7},{9,8},{10,9... | collective-permute-start | bytes 1544 | tf_op jit(solution)/shard_map/ppermute | solution.py:21
  60.9 1.9 collective-permute-start.6
  63.1 6.7 %collective-permute-start.13 = (s32[1,128]{1,0:T(1,128)S(1)}, s32[1,128]{1,0:T(1,128)S(1)}, u32[]{:S(2)}, u32[]{:S(2)}) collective-permute-start(s32[1,128]{1,0:T(1,128)S(1)} %collective-permute-done.12), channel_id=1, source_target_pairs={{0,15},{1,0},{2,1},{3,2},{4,3},{5,4},{6,5},{7,6},{8,7},{9,8},{10,9... | collective-permute-start | bytes 1544 | tf_op jit(solution)/shard_map/ppermute | solution.py:21
  69.8 1.9 collective-permute-start.7
  72.7 6.7 %collective-permute-start.14 = (s32[1,128]{1,0:T(1,128)S(1)}, s32[1,128]{1,0:T(1,128)S(1)}, u32[]{:S(2)}, u32[]{:S(2)}) collective-permute-start(s32[1,128]{1,0:T(1,128)S(1)} %collective-permute-done.13), channel_id=1, source_target_pairs={{0,15},{1,0},{2,1},{3,2},{4,3},{5,4},{6,5},{7,6},{8,7},{9,8},{10,9... | collective-permute-start | bytes 1544 | tf_op jit(solution)/shard_map/ppermute | solution.py:21
  81.8 6.2 %all-to-all-start.1 = ((bf16[128,16,128]{0,2,1:T(8,128)(2,1)}), bf16[128,16,128]{0,2,1:T(8,128)(2,1)S(1)}, u32[]{:S(2)}, u32[]{:S(2)}) async-start(bf16[128,16,128]{0,2,1:T(8,128)(2,1)} %bitcast.12), calls=%async_computation.1 | async-start | bytes 1048576 | tf_op jit(solution)/shard_map/all_to_all | solution.py:173
  90.1 6.9 %all-to-all-done.1 = bf16[128,16,128]{0,2,1:T(8,128)(2,1)S(1)} async-done(((bf16[128,16,128]{0,2,1:T(8,128)(2,1)}), bf16[128,16,128]{0,2,1:T(8,128)(2,1)S(1)}, u32[]{:S(2)}, u32[]{:S(2)}) %all-to-all-start.1) | async-done | bytes 524320 | tf_op jit(solution)/shard_map/all_to_all | solution.py:173
  98.0 3.6 all-to-all-start.2
  103.5 10.4 %all-to-all-done.2 = bf16[128,16,128]{2,0,1:T(8,128)(2,1)S(1)} async-done(((bf16[128,16,128]{2,0,1:T(8,128)(2,1)}), bf16[128,16,128]{2,0,1:T(8,128)(2,1)S(1)}, u32[]{:S(2)}, u32[]{:S(2)}) %all-to-all-start.2) | async-done | bytes 524320 | tf_op jit(solution)/shard_map/all_to_all | solution.py:174
  113.9 4.2 %all-to-all-start.3 = ((bf16[128,16,128]{2,0,1:T(8,128)(2,1)}), bf16[128,16,128]{2,0,1:T(8,128)(2,1)}, u32[]{:S(2)}, u32[]{:S(2)}) async-start(bf16[128,16,128]{2,0,1:T(8,128)(2,1)} %bitcast.129), calls=%async_computation.3 | async-start | bytes 1048576 | tf_op jit(solution)/shard_map/all_to_all | solution.py:172
  118.1 3.1 fusion.63
  122.3 6.4 %all-to-all-done.3 = bf16[128,16,128]{2,0,1:T(8,128)(2,1)} async-done(((bf16[128,16,128]{2,0,1:T(8,128)(2,1)}), bf16[128,16,128]{2,0,1:T(8,128)(2,1)}, u32[]{:S(2)}, u32[]{:S(2)}) %all-to-all-start.3) | async-done | bytes 524320 | tf_op jit(solution)/shard_map/all_to_all | solution.py:172
  130.0 69.0 %while.79 = (s32[]{:T(128)}, f32[2048,128]{0,1:T(8,128)}, f32[2048,128]{1,0:T(8,128)S(1)}, f32[2048,128]{1,0:T(8,128)S(1)}, bf16[2048,1,128]{0,2,1:T(8,128)(2,1)...) while((s32[]{:T(128)}, f32[2048,128]{0,1:T(8,128)}, ...), condition=%wide.region_12.13_spmd, body=%wide.region_5.12_spmd.sunk | while | flops 475268608 | bytes 14478353 | solution.py:152
  130.9 1.9 while.80
  131.0 1.4 fusion.101
  133.9 3.7 %while.81 = (s32[]{:T(128)}, f32[512,128]{1,0:T(8,128)S(1)}, f32[2048,128]{1,0:T(8,128)S(1)}, f32[2048,128]{1,0:T(8,128)S(1)}, s32[]{:T(128)}, /*index=5*/s32[51...) while((s32[]{:T(128)}, f32[512,128]{1,0:T(8,128)S(1)}, ...), condition=%wide.region_11.11_spmd.clone, body=%wide.region_10.10_spmd.clone.sunk | while | flops 338887680 | bytes 5656819 | solution.py:138
  134.0 1.4 fusion.112
  136.3 1.3 convolution_add_fusion.7
  139.8 3.7 %while.80 = (s32[]{:T(128)}, f32[512]{0:T(512)S(1)}, f32[512,128]{1,0:T(8,128)S(1)}, s32[]{:T(128)}, s32[512]{0:T(512)S(1)}, /*index=5*/s32[2048]{0:T(1024)S(1)}...) while((s32[]{:T(128)}, f32[512]{0:T(512)S(1)}, ...), condition=%wide.region_8.8_spmd.clone, body=%wide.region_6.7_spmd.clone.sunk | while | flops 136119296 | bytes 1990855 | solution.py:95
  139.9 1.4 fusion.101
  141.7 1.4 fusion.101
  144.7 7.4 %while.81 = (s32[]{:T(128)}, f32[512,128]{1,0:T(8,128)S(1)}, f32[2048,128]{1,0:T(8,128)S(1)}, f32[2048,128]{1,0:T(8,128)S(1)}, s32[]{:T(128)}, /*index=5*/s32[51...) while((s32[]{:T(128)}, f32[512,128]{1,0:T(8,128)S(1)}, ...), condition=%wide.region_11.11_spmd.clone, body=%wide.region_10.10_spmd.clone.sunk | while | flops 338887680 | bytes 5656819 | solution.py:138
  144.8 1.4 fusion.112
  148.5 1.4 fusion.112
  154.2 5.6 %while.80 = (s32[]{:T(128)}, f32[512]{0:T(512)S(1)}, f32[512,128]{1,0:T(8,128)S(1)}, s32[]{:T(128)}, s32[512]{0:T(512)S(1)}, /*index=5*/s32[2048]{0:T(1024)S(1)}...) while((s32[]{:T(128)}, f32[512]{0:T(512)S(1)}, ...), condition=%wide.region_8.8_spmd.clone, body=%wide.region_6.7_spmd.clone.sunk | while | flops 136119296 | bytes 1990855 | solution.py:95
  154.3 1.4 fusion.101
  156.2 1.4 fusion.101
  158.1 1.4 fusion.101
  161.0 11.1 %while.81 = (s32[]{:T(128)}, f32[512,128]{1,0:T(8,128)S(1)}, f32[2048,128]{1,0:T(8,128)S(1)}, f32[2048,128]{1,0:T(8,128)S(1)}, s32[]{:T(128)}, /*index=5*/s32[51...) while((s32[]{:T(128)}, f32[512,128]{1,0:T(8,128)S(1)}, ...), condition=%wide.region_11.11_spmd.clone, body=%wide.region_10.10_spmd.clone.sunk | while | flops 338887680 | bytes 5656819 | solution.py:138
  161.1 1.4 fusion.112
  164.8 1.4 fusion.112
  168.5 1.4 fusion.112
  174.3 7.5 %while.80 = (s32[]{:T(128)}, f32[512]{0:T(512)S(1)}, f32[512,128]{1,0:T(8,128)S(1)}, s32[]{:T(128)}, s32[512]{0:T(512)S(1)}, /*index=5*/s32[2048]{0:T(1024)S(1)}...) while((s32[]{:T(128)}, f32[512]{0:T(512)S(1)}, ...), condition=%wide.region_8.8_spmd.clone, body=%wide.region_6.7_spmd.clone.sunk | while | flops 136119296 | bytes 1990855 | solution.py:95
  174.4 1.4 fusion.101
  176.2 1.4 fusion.101
  178.1 1.4 fusion.101
  180.0 1.4 fusion.101
  182.9 14.8 %while.81 = (s32[]{:T(128)}, f32[512,128]{1,0:T(8,128)S(1)}, f32[2048,128]{1,0:T(8,128)S(1)}, f32[2048,128]{1,0:T(8,128)S(1)}, s32[]{:T(128)}, /*index=5*/s32[51...) while((s32[]{:T(128)}, f32[512,128]{1,0:T(8,128)S(1)}, ...), condition=%wide.region_11.11_spmd.clone, body=%wide.region_10.10_spmd.clone.sunk | while | flops 338887680 | bytes 5656819 | solution.py:138
  183.0 1.4 fusion.112
  186.7 1.4 fusion.112
  190.5 1.4 fusion.112
  194.2 1.4 fusion.112
  196.5 1.3 convolution_add_fusion.7
  199.0 1.3 copy.139
  200.4 4.1 %fusion.60 = (f32[2048,1,64]{0,2,1:T(8,128)S(1)}, f32[2048,1,64]{0,2,1:T(8,128)S(1)}, f32[2048,1,64]{0,2,1:T(8,128)S(1)}, f32[2048,1,64]{0,2,1:T(8,128)S(1)}) fusion(f32[2048,1,128]{0,2,1:T(8,128)} %bitcast.158, f32[64]{0:T(128)S(1)} %negate_power_fusion, f32[2048]{0:T(1024)S(1)} %convert_multiply_fusion.1, f32[2048,1,128]{0,2,1:T(8,128)} %bitcast.157), kind=kLoop, calls=%fused_computation.89 | loop fusion | flops 1966080 | bytes 4202752 | tf_op jit(solution)/shard_map/transpose(jvp())/add_any | solution.py:47
  209.2 3.6 all-to-all-start.4
  215.0 6.8 %all-to-all-done.4 = bf16[16,2,8192]{2,1,0:T(2,128)(2,1)S(1)} async-done(((bf16[16,2,8192]{2,1,0:T(2,128)(2,1)}), bf16[16,2,8192]{2,1,0:T(2,128)(2,1)S(1)}, u32[]{:S(2)}, u32[]{:S(2)}) %all-to-all-start.4) | async-done | bytes 524320 | tf_op jit(solution)/shard_map/all_to_all | solution.py:191
  221.8 3.8 %all-to-all-start.5 = ((bf16[16,2,8192]{2,1,0:T(2,128)(2,1)}), bf16[16,2,8192]{2,1,0:T(2,128)(2,1)S(1)}, u32[]{:S(2)}, u32[]{:S(2)}) async-start(bf16[16,2,8192]{2,1,0:T(2,128)(2,1)} %reshape.578), calls=%async_computation.5 | async-start | bytes 1048576 | tf_op jit(solution)/shard_map/all_to_all | solution.py:194
  227.5 6.9 %all-to-all-done.5 = bf16[16,2,8192]{2,1,0:T(2,128)(2,1)S(1)} async-done(((bf16[16,2,8192]{2,1,0:T(2,128)(2,1)}), bf16[16,2,8192]{2,1,0:T(2,128)(2,1)S(1)}, u32[]{:S(2)}, u32[]{:S(2)}) %all-to-all-start.5) | async-done | bytes 524320 | tf_op jit(solution)/shard_map/all_to_all | solution.py:194
  234.4 3.6 all-to-all-start.6
  238.0 120.6 %all-reduce.4 = (f32[128]{0:T(128)}, f32[128]{0:T(128)}) all-reduce(f32[128]{0:T(128)S(1)} %get-tuple-element.430, f32[128]{0:T(128)S(1)} %get-tuple-element.428), channel_id=1, replica_groups=mesh['dp'=32,'seq'=16] {'dp','seq'}, use_global_device_ids=true, to_apply=%region_18.19 | all-reduce | flops 256 | bytes 2048 | tf_op jit(solution)/shard_map/psum | solution.py:206
  (278 shorter events, 62.5 us)
Async XLA Ops:
  0.6 8.7 %collective-permute-start = (s32[1,128]{1,0:T(1,128)}, s32[1,128]{1,0:T(1,128)S(1)}, u32[]{:S(2)}, u32[]{:S(2)}) collective-permute-start(s32[1,128]{1,0:T(1,128)} %param.17), channel_id=1, source_target_pairs={{0,1},{1,2},{2,3},{3,4},{4,5},{5,6},{6,7},{7,8},{8,9},{9,10},{10,1... | collective-permute-start | bytes 1544 | tf_op jit(solution)/shard_map/ppermute | solution.py:19
  9.4 8.6 %collective-permute-start.1 = (s32[1,128]{1,0:T(1,128)S(1)}, s32[1,128]{1,0:T(1,128)S(1)}, u32[]{:S(2)}, u32[]{:S(2)}) collective-permute-start(s32[1,128]{1,0:T(1,128)S(1)} %collective-permute-done), channel_id=1, source_target_pairs={{0,1},{1,2},{2,3},{3,4},{4,5},{5,6},{6,7},{7,8},{8,9},{9,10},{10,1... | collective-permute-start | bytes 1544 | tf_op jit(solution)/shard_map/ppermute | solution.py:19
  11.3 16.9 %collective-permute-start.8 = (s32[1,128]{1,0:T(1,128)}, s32[1,128]{1,0:T(1,128)S(1)}, u32[]{:S(2)}, u32[]{:S(2)}) collective-permute-start(s32[1,128]{1,0:T(1,128)} %param.17), channel_id=1, source_target_pairs={{0,15},{1,0},{2,1},{3,2},{4,3},{5,4},{6,5},{7,6},{8,7},{9,8},{10,9... | collective-permute-start | bytes 1544 | tf_op jit(solution)/shard_map/ppermute | solution.py:21
  18.0 16.8 %collective-permute-start.2 = (s32[1,128]{1,0:T(1,128)S(1)}, s32[1,128]{1,0:T(1,128)S(1)}, u32[]{:S(2)}, u32[]{:S(2)}) collective-permute-start(s32[1,128]{1,0:T(1,128)S(1)} %collective-permute-done.1), channel_id=1, source_target_pairs={{0,1},{1,2},{2,3},{3,4},{4,5},{5,6},{6,7},{7,8},{8,9},{9,10},{10,1... | collective-permute-start | bytes 1544 | tf_op jit(solution)/shard_map/ppermute | solution.py:19
  21.9 41.0 %copy-start.9 = (bf16[1,128,8,128]{3,2,1,0:T(8,128)(2,1)S(1)}, bf16[1,128,8,128]{3,2,1,0:T(8,128)(2,1)}, u32[]{:S(2)}) copy-start(bf16[1,128,8,128]{3,2,1,0:T(8,128)(2,1)} %param.14) | copy-start | bytes 786436
  21.9 59.0 %all-to-all-start = ((bf16[128,16,128]{2,0,1:T(8,128)(2,1)}), bf16[128,16,128]{2,0,1:T(8,128)(2,1)S(1)}, u32[]{:S(2)}, u32[]{:S(2)}) async-start(bf16[128,16,128]{2,0,1:T(8,128)(2,1)} %bitcast.130), calls=%async_computation | async-start | bytes 1048576 | tf_op jit(solution)/shard_map/all_to_all | solution.py:171
  28.2 8.6 %collective-permute-start.9 = (s32[1,128]{1,0:T(1,128)S(1)}, s32[1,128]{1,0:T(1,128)S(1)}, u32[]{:S(2)}, u32[]{:S(2)}) collective-permute-start(s32[1,128]{1,0:T(1,128)S(1)} %collective-permute-done.8), channel_id=1, source_target_pairs={{0,15},{1,0},{2,1},{3,2},{4,3},{5,4},{6,5},{7,6},{8,7},{9,8},{10,9... | collective-permute-start | bytes 1544 | tf_op jit(solution)/shard_map/ppermute | solution.py:21
  34.8 8.7 %collective-permute-start.3 = (s32[1,128]{1,0:T(1,128)S(1)}, s32[1,128]{1,0:T(1,128)S(1)}, u32[]{:S(2)}, u32[]{:S(2)}) collective-permute-start(s32[1,128]{1,0:T(1,128)S(1)} %collective-permute-done.2), channel_id=1, source_target_pairs={{0,1},{1,2},{2,3},{3,4},{4,5},{5,6},{6,7},{7,8},{8,9},{9,10},{10,1... | collective-permute-start | bytes 1544 | tf_op jit(solution)/shard_map/ppermute | solution.py:19
  36.8 8.6 %collective-permute-start.10 = (s32[1,128]{1,0:T(1,128)S(1)}, s32[1,128]{1,0:T(1,128)S(1)}, u32[]{:S(2)}, u32[]{:S(2)}) collective-permute-start(s32[1,128]{1,0:T(1,128)S(1)} %collective-permute-done.9), channel_id=1, source_target_pairs={{0,15},{1,0},{2,1},{3,2},{4,3},{5,4},{6,5},{7,6},{8,7},{9,8},{10,9... | collective-permute-start | bytes 1544 | tf_op jit(solution)/shard_map/ppermute | solution.py:21
  43.5 8.8 %collective-permute-start.4 = (s32[1,128]{1,0:T(1,128)S(1)}, s32[1,128]{1,0:T(1,128)S(1)}, u32[]{:S(2)}, u32[]{:S(2)}) collective-permute-start(s32[1,128]{1,0:T(1,128)S(1)} %collective-permute-done.3), channel_id=1, source_target_pairs={{0,1},{1,2},{2,3},{3,4},{4,5},{5,6},{6,7},{7,8},{8,9},{9,10},{10,1... | collective-permute-start | bytes 1544 | tf_op jit(solution)/shard_map/ppermute | solution.py:19
  45.4 26.3 %copy-start.10 = (bf16[1,128,8,128]{3,2,1,0:T(8,128)(2,1)S(1)}, bf16[1,128,8,128]{3,2,1,0:T(8,128)(2,1)}, u32[]{:S(2)}) copy-start(bf16[1,128,8,128]{3,2,1,0:T(8,128)(2,1)} %param.15) | copy-start | bytes 786436
  45.4 8.8 %collective-permute-start.11 = (s32[1,128]{1,0:T(1,128)S(1)}, s32[1,128]{1,0:T(1,128)S(1)}, u32[]{:S(2)}, u32[]{:S(2)}) collective-permute-start(s32[1,128]{1,0:T(1,128)S(1)} %collective-permute-done.10), channel_id=1, source_target_pairs={{0,15},{1,0},{2,1},{3,2},{4,3},{5,4},{6,5},{7,6},{8,7},{9,8},{10,9... | collective-permute-start | bytes 1544 | tf_op jit(solution)/shard_map/ppermute | solution.py:21
  52.2 8.6 %collective-permute-start.5 = (s32[1,128]{1,0:T(1,128)S(1)}, s32[1,128]{1,0:T(1,128)S(1)}, u32[]{:S(2)}, u32[]{:S(2)}) collective-permute-start(s32[1,128]{1,0:T(1,128)S(1)} %collective-permute-done.4), channel_id=1, source_target_pairs={{0,1},{1,2},{2,3},{3,4},{4,5},{5,6},{6,7},{7,8},{8,9},{9,10},{10,1... | collective-permute-start | bytes 1544 | tf_op jit(solution)/shard_map/ppermute | solution.py:19
  54.2 8.9 %collective-permute-start.12 = (s32[1,128]{1,0:T(1,128)S(1)}, s32[1,128]{1,0:T(1,128)S(1)}, u32[]{:S(2)}, u32[]{:S(2)}) collective-permute-start(s32[1,128]{1,0:T(1,128)S(1)} %collective-permute-done.11), channel_id=1, source_target_pairs={{0,15},{1,0},{2,1},{3,2},{4,3},{5,4},{6,5},{7,6},{8,7},{9,8},{10,9... | collective-permute-start | bytes 1544 | tf_op jit(solution)/shard_map/ppermute | solution.py:21
  60.9 8.9 %collective-permute-start.6 = (s32[1,128]{1,0:T(1,128)S(1)}, s32[1,128]{1,0:T(1,128)S(1)}, u32[]{:S(2)}, u32[]{:S(2)}) collective-permute-start(s32[1,128]{1,0:T(1,128)S(1)} %collective-permute-done.5), channel_id=1, source_target_pairs={{0,1},{1,2},{2,3},{3,4},{4,5},{5,6},{6,7},{7,8},{8,9},{9,10},{10,1... | collective-permute-start | bytes 1544 | tf_op jit(solution)/shard_map/ppermute | solution.py:19
  62.8 8.9 %copy-start.8 = (bf16[1,128,16,128]{3,2,1,0:T(8,128)(2,1)S(1)}, bf16[1,128,16,128]{3,2,1,0:T(8,128)(2,1)}, u32[]{:S(2)}) copy-start(bf16[1,128,16,128]{3,2,1,0:T(8,128)(2,1)} %param.16) | copy-start | bytes 1572868
  63.1 9.6 %collective-permute-start.13 = (s32[1,128]{1,0:T(1,128)S(1)}, s32[1,128]{1,0:T(1,128)S(1)}, u32[]{:S(2)}, u32[]{:S(2)}) collective-permute-start(s32[1,128]{1,0:T(1,128)S(1)} %collective-permute-done.12), channel_id=1, source_target_pairs={{0,15},{1,0},{2,1},{3,2},{4,3},{5,4},{6,5},{7,6},{8,7},{9,8},{10,9... | collective-permute-start | bytes 1544 | tf_op jit(solution)/shard_map/ppermute | solution.py:21
  69.8 9.6 %collective-permute-start.7 = (s32[1,128]{1,0:T(1,128)S(1)}, s32[1,128]{1,0:T(1,128)S(1)}, u32[]{:S(2)}, u32[]{:S(2)}) collective-permute-start(s32[1,128]{1,0:T(1,128)S(1)} %collective-permute-done.6), channel_id=1, source_target_pairs={{0,1},{1,2},{2,3},{3,4},{4,5},{5,6},{6,7},{7,8},{8,9},{9,10},{10,1... | collective-permute-start | bytes 1544 | tf_op jit(solution)/shard_map/ppermute | solution.py:19
  72.7 7.5 %collective-permute-start.14 = (s32[1,128]{1,0:T(1,128)S(1)}, s32[1,128]{1,0:T(1,128)S(1)}, u32[]{:S(2)}, u32[]{:S(2)}) collective-permute-start(s32[1,128]{1,0:T(1,128)S(1)} %collective-permute-done.13), channel_id=1, source_target_pairs={{0,15},{1,0},{2,1},{3,2},{4,3},{5,4},{6,5},{7,6},{8,7},{9,8},{10,9... | collective-permute-start | bytes 1544 | tf_op jit(solution)/shard_map/ppermute | solution.py:21
  79.5 0.7 copy-start.13
  81.8 15.2 %all-to-all-start.1 = ((bf16[128,16,128]{0,2,1:T(8,128)(2,1)}), bf16[128,16,128]{0,2,1:T(8,128)(2,1)S(1)}, u32[]{:S(2)}, u32[]{:S(2)}) async-start(bf16[128,16,128]{0,2,1:T(8,128)(2,1)} %bitcast.12), calls=%async_computation.1 | async-start | bytes 1048576 | tf_op jit(solution)/shard_map/all_to_all | solution.py:173
  88.5 0.7 copy-start.12
  89.2 1.0 copy-start
  97.0 4.7 %copy-start.2 = (bf16[128,16,128]{0,2,1:T(8,128)(2,1)}, bf16[128,16,128]{0,2,1:T(8,128)(2,1)S(1)}, u32[]{:S(2)}) copy-start(bf16[128,16,128]{0,2,1:T(8,128)(2,1)S(1)} %all-to-all-done.1) | copy-start | bytes 1572868
  98.0 15.9 %all-to-all-start.2 = ((bf16[128,16,128]{2,0,1:T(8,128)(2,1)}), bf16[128,16,128]{2,0,1:T(8,128)(2,1)S(1)}, u32[]{:S(2)}, u32[]{:S(2)}) async-start(bf16[128,16,128]{2,0,1:T(8,128)(2,1)} %bitcast.20), calls=%async_computation.2 | async-start | bytes 1048576 | tf_op jit(solution)/shard_map/all_to_all | solution.py:174
  101.7 0.7 copy-start.11
  103.5 14.6 %copy-start.4 = (f32[2048,1,128]{0,2,1:T(8,128)S(1)}, f32[2048,1,128]{0,2,1:T(8,128)}, u32[]{:S(2)}) copy-start(f32[2048,1,128]{0,2,1:T(8,128)} %fusion.33) | copy-start | bytes 3145732
  113.9 14.8 %all-to-all-start.3 = ((bf16[128,16,128]{2,0,1:T(8,128)(2,1)}), bf16[128,16,128]{2,0,1:T(8,128)(2,1)}, u32[]{:S(2)}, u32[]{:S(2)}) async-start(bf16[128,16,128]{2,0,1:T(8,128)(2,1)} %bitcast.129), calls=%async_computation.3 | async-start | bytes 1048576 | tf_op jit(solution)/shard_map/all_to_all | solution.py:172
  121.2 1.0 copy-start.7
  130.0 0.8 copy-start.5
  137.8 1.1 copy-start.6
  138.9 0.8 copy-start.5
  152.2 1.1 copy-start.6
  153.4 0.8 copy-start.5
  172.3 1.1 copy-start.6
  173.4 0.8 copy-start.5
  197.9 1.1 copy-start.6
  200.4 4.1 %copy-start.3 = (bf16[128,16,128]{0,2,1:T(8,128)(2,1)S(1)}, bf16[128,16,128]{0,2,1:T(8,128)(2,1)}, u32[]{:S(2)}) copy-start(bf16[128,16,128]{0,2,1:T(8,128)(2,1)} %copy-done.2) | copy-start | bytes 1572868
  204.4 1.2 copy-start.1
  209.2 12.5 %all-to-all-start.4 = ((bf16[16,2,8192]{2,1,0:T(2,128)(2,1)}), bf16[16,2,8192]{2,1,0:T(2,128)(2,1)S(1)}, u32[]{:S(2)}, u32[]{:S(2)}) async-start(bf16[16,2,8192]{2,1,0:T(2,128)(2,1)} %reshape.576), calls=%async_computation.4 | async-start | bytes 1048576 | tf_op jit(solution)/shard_map/all_to_all | solution.py:191
  221.8 12.7 %all-to-all-start.5 = ((bf16[16,2,8192]{2,1,0:T(2,128)(2,1)}), bf16[16,2,8192]{2,1,0:T(2,128)(2,1)S(1)}, u32[]{:S(2)}, u32[]{:S(2)}) async-start(bf16[16,2,8192]{2,1,0:T(2,128)(2,1)} %reshape.578), calls=%async_computation.5 | async-start | bytes 1048576 | tf_op jit(solution)/shard_map/all_to_all | solution.py:194
  234.4 127.6 %all-to-all-start.6 = ((bf16[16,2,8192]{2,1,0:T(2,128)(2,1)}), bf16[16,2,8192]{2,1,0:T(2,128)(2,1)S(1)}, u32[]{:S(2)}, u32[]{:S(2)}) async-start(bf16[16,2,8192]{2,1,0:T(2,128)(2,1)} %reshape.580), calls=%async_computation.6 | async-start | bytes 1048576 | tf_op jit(solution)/shard_map/all_to_all | solution.py:197
